TPU v7x, 32 devices: a whole 2x2x4 slice. The times are simulated.
32 devices in a mesh: comp: 2 (over core), gx: 4 (over y, x), gy: 4 (over z).
Axes of the slice: x: 2, y: 2, z: 4, core: 2. Of those that a mesh axis runs over, the one named last changes fastest.
Arguments:
- state: float32 [2, 8, 96, 3072], P('comp', None, 'gx', 'gy'), may hold values from -6 to 6
- response: float32 [2, 8, 3072], P('comp'), may hold values from -0.95 to 0
- diffusion: float32 [2, 96, 3072], P('comp', 'gx', 'gy'), may hold values from 0.02 to 0.24
- land_mask: int32 [96, 3072], P('gx', 'gy'), may hold values 0 or 1
- couple_src: int32 [2, 4, 4, 16, 128], P('comp', 'gx', 'gy'), may hold values from 0 to 18431
- couple_dst: int32 [2, 4, 4, 16, 128], P('comp', 'gx', 'gy'), may hold values from 0 to 18431
- couple_weight: float32 [2, 4, 4, 16, 128], P('comp', 'gx', 'gy'), may hold values from 0.1 to 1
- couple_count: int32 [2, 4, 4, 16], P('comp', 'gx', 'gy'), may hold values from 0 to 128, as said below
Outputs:
- final_state: float32 [2, 8, 96, 3072], P('comp', None, 'gx', 'gy')
Inputs may be any that keep to these rules, and one draw needn't show every extreme that they name: `couple_count`: at most 128 live slots per ordered device pair; every sending device has one pair with exactly 128.
All inputs are finite; a program needn't handle non-finite values. No bound on the sum of `land_mask` on one device may be relied on, other than what follows from the above.
Results may differ from a plain program's by a relative error of at most 0.0095.
Values may be sent and summed in bfloat16 or wider, within the bound.
A program may use at most 128 MiB of HBM per device.

v0:
```python
import math
import jax
import jax.numpy as jnp
from jax import lax
from jax.sharding import PartitionSpec as P

FC = 4


def extended(block, sides, width):
    for axis, dim in sides:
        count = lax.axis_size(axis)
        forward = [(i, i + 1) for i in range(count - 1)]
        backward = [(target, source) for source, target in forward]
        low = lax.ppermute(
            lax.slice_in_dim(block, block.shape[dim] - width, None, axis=dim), axis, forward
        )
        high = lax.ppermute(lax.slice_in_dim(block, 0, width, axis=dim), axis, backward)
        block = jnp.concatenate([low, block, high], axis=dim)
    return block


def partner(value, axis, stride):
    mask = 2**stride
    pairs = [(source, source ^ mask) for source in range(lax.axis_size(axis))]
    return lax.ppermute(value, axis, pairs)


def make_table(cols):
    rows_idx = jnp.arange(cols, dtype=jnp.int32)[:, None]
    wave_idx = jnp.arange(cols // 2, dtype=jnp.int32)[None, :]
    phase = rows_idx * wave_idx % cols
    angle = phase.astype(jnp.float32) * (2.0 * math.pi / cols)
    return jnp.concatenate([jnp.cos(angle), jnp.sin(angle)], axis=1).astype(jnp.bfloat16)


def back_transform(filtered, table_part):
    return lax.dot_general(
        filtered, table_part, (((1,), (1,)), ((), ())), preferred_element_type=jnp.float32
    )


def circle_increment(circles, resp_part, table, scale):
    count, rows_part, cols_all = circles.shape
    spec = jnp.dot(circles.reshape(-1, cols_all), table, preferred_element_type=jnp.float32)
    spec = spec.reshape(count, rows_part, cols_all)
    filtered = (spec * resp_part[:, None, :]).astype(jnp.bfloat16)
    incr = (back_transform(filtered.reshape(-1, cols_all), table) * scale).astype(jnp.bfloat16)
    return incr.reshape(count, rows_part, cols_all)


def diffuse(fields, rate):
    padded = extended(fields.astype(jnp.bfloat16), (("gx", 1),), 1).astype(fields.dtype)
    return fields + rate[None] * (padded[:, 2:] + padded[:, :-2] - 2.0 * fields)


def local(
    state, response, diffusion, land_mask, couple_src, couple_dst, couple_weight, couple_count
):
    levels, rows_dev, cols_dev = (state.shape[1], state.shape[2], state.shape[3])
    groups_x = lax.axis_size("gx")
    groups_y = lax.axis_size("gy")
    peers = groups_x * groups_y
    slots = couple_src.shape[4]
    cells = rows_dev * cols_dev
    cols_all = cols_dev * groups_y
    per_level = levels // groups_y
    section = lax.axis_index("comp")
    keep = jnp.where(section == 1, land_mask.astype(jnp.float32), jnp.float32(1.0))
    table = make_table(cols_all)
    scale = 2.0 / cols_all
    src_idx = couple_src.reshape(peers, slots)
    dst_idx = couple_dst.reshape(peers, slots)
    live = jnp.arange(slots, dtype=jnp.int32)[None, :] < couple_count.reshape(peers, 1)
    weights = jnp.where(live, couple_weight.reshape(peers, slots), jnp.float32(0.0))
    first_level = lax.axis_index("gy") * per_level
    resp_mine = lax.dynamic_slice_in_dim(response[0], first_level, per_level, 0)
    rate = diffusion[0]
    fields = state[0]
    surface = fields[:FC].reshape(FC, cells)
    outgoing = jnp.transpose(surface[:, src_idx] * weights[None], (1, 0, 2))
    crossed = partner(outgoing, "comp", 0)
    arrived = lax.all_to_all(crossed, ("gx", "gy"), split_axis=0, concat_axis=0, tiled=True)
    incoming = jnp.transpose(arrived, (1, 0, 2))
    surface = surface.at[:, dst_idx].add(incoming)
    surf = surface.reshape(FC, rows_dev, cols_dev)
    fields = jnp.concatenate([surf, fields[FC:]], axis=0)
    grid_bf = fields.astype(jnp.bfloat16)
    circles = lax.all_to_all(grid_bf, "gy", split_axis=0, concat_axis=2, tiled=True)
    incr = circle_increment(circles, resp_mine, table, scale)
    incr = lax.all_to_all(incr, "gy", split_axis=2, concat_axis=0, tiled=True)
    fields = fields + incr.astype(jnp.float32)
    fields = diffuse(fields, rate) * keep[None]
    return fields[None]


def solution(mesh):
    return jax.shard_map(
        local,
        mesh=mesh,
        in_specs=(
            P("comp", None, "gx", "gy"),
            P("comp", None, None),
            P("comp", "gx", "gy"),
            P("gx", "gy"),
            P("comp", "gx", "gy", None, None),
            P("comp", "gx", "gy", None, None),
            P("comp", "gx", "gy", None, None),
            P("comp", "gx", "gy", None),
        ),
        out_specs=P("comp", None, "gx", "gy"),
        check_vma=False,
    )
```

profile of v0, /device:TPU:4, one launch (start us, length us, event | category | flops | bytes accessed | tf_op | source)
XLA Modules:
  0.0 198.0 jit_solution(5701691548152781341)
XLA Ops:
  0.0 0.0 copy-start
  0.0 0.0 copy-start.2
  0.0 0.0 copy-start.3
  0.0 0.0 copy-start.5
  0.0 0.0 copy-start.4
  0.0 1.1 fusion.28
  1.2 0.0 copy-start.1
  1.2 5.6 %copy.20 = f32[1,4,24,768]{1,3,2,0:T(8,128)} copy(f32[1,4,24,768]{3,2,1,0:T(8,128)S(1)} %get-tuple-element.5) | data formatting | bytes 589824 | tf_op jit(solution)/shard_map/slice | solution.py:80
  6.8 0.0 copy-done.2
  6.8 9.1 %gather_fusion = f32[2048,4]{1,0:T(8,128)S(1)} fusion(f32[4,18432]{0,1:T(8,128)} %bitcast.55, s32[2048]{0:T(1024)S(1)} %fusion.25), kind=kCustom, calls=%fused_computation | custom fusion | bytes 73728 | tf_op jit(solution)/shard_map/gather | solution.py:81
  16.0 0.3 copy.21
  16.3 0.0 copy-done.3
  16.3 0.0 copy-done.5
  16.3 0.1 bitcast_select_fusion
  16.4 0.1 collective-permute-start
  16.5 1.2 collective-permute-done
  17.7 0.6 copy.22
  18.3 7.3 %all-to-all-start = ((f32[16,4,128]{2,1,0:T(4,128)}), f32[16,4,128]{2,1,0:T(4,128)S(1)}, u32[]{:S(2)}, u32[]{:S(2)}) async-start(f32[16,4,128]{2,1,0:T(4,128)} %copy.22), calls=%async_computation | async-start | bytes 65536 | tf_op jit(solution)/shard_map/all_to_all | solution.py:83
  25.6 0.0 copy-done.4
  25.6 6.1 %all-to-all-done = f32[16,4,128]{2,1,0:T(4,128)S(1)} async-done(((f32[16,4,128]{2,1,0:T(4,128)}), f32[16,4,128]{2,1,0:T(4,128)S(1)}, u32[]{:S(2)}, u32[]{:S(2)}) %all-to-all-start) | async-done | bytes 32800 | tf_op jit(solution)/shard_map/all_to_all | solution.py:83
  31.7 0.4 copy.23
  32.0 17.6 %scatter_fusion = f32[4,18432]{0,1:T(8,128)} fusion(f32[4,18432]{0,1:T(8,128)} %bitcast.56, s32[2048]{0:T(1024)S(1)} %fusion.23, f32[2048,4]{1,0:T(8,128)S(1)} %copy.23), kind=kCustom, calls=%fused_computation.1 | custom fusion | flops 8192 | bytes 106496 | tf_op jit(solution)/shard_map/scatter-add | solution.py:85
  49.7 6.4 %copy.24 = f32[4,24,768]{2,1,0:T(8,128)S(1)} copy(f32[4,24,768]{0,2,1:T(8,128)} %bitcast.57) | data formatting | bytes 589824 | tf_op jit(solution)/shard_map/reshape | solution.py:86
  56.1 0.0 copy-done.1
  56.1 0.7 fusion.21
  56.8 3.5 %all-to-all-start.1 = ((bf16[8,24,768]{2,1,0:T(8,128)(2,1)}), bf16[8,24,768]{2,1,0:T(8,128)(2,1)S(1)}, u32[]{:S(2)}, u32[]{:S(2)}) async-start(bf16[8,24,768]{2,1,0:T(8,128)(2,1)} %fusion.21), calls=%async_computation.1 | async-start | bytes 589824 | tf_op jit(solution)/shard_map/all_to_all | solution.py:89
  60.3 79.5 %sine_convert_fusion = (bf16[3072,1536]{1,0:T(8,128)(2,1)}, bf16[3072,1536]{1,0:T(8,128)(2,1)}) fusion(), kind=kLoop, calls=%fused_computation.8 | loop fusion | flops 51904512 | bytes 18874368 | tf_op jit(solution)/shard_map/convert.4
  139.8 0.0 copy-done
  139.8 0.0 all-to-all-done.1
  139.8 0.2 copy.29
  140.0 0.2 dot_general.8
  140.2 8.2 %fusion.12 = bf16[2,24,3072]{2,1,0:T(8,128)(2,1)S(1)} fusion(bf16[2,24,3072]{2,1,0:T(8,128)(2,1)S(1)} %dot_general.8, bf16[3072,1536]{1,0:T(8,128)(2,1)} %get-tuple-element.9, bf16[3072,1536]{1,0:T(8,128)(2,1)} %get-tuple-element.10, f32[2,3072]{1,0:T(2,128)S(1)} %dynamic-slice_bitcast_fusion), kind=kOutput, calls=%fused_computation.17 | convolution fusion | flops 944013312 | bytes 19488768 | tf_op jit(solution)/shard_map/dot_general | solution.py:45
  148.4 9.6 %fusion.15 = bf16[48,3072]{1,0:T(8,128)(2,1)S(1)} fusion(bf16[48,3072]{1,0:T(8,128)(2,1)S(1)} %bitcast.67, bf16[3072,1536]{1,0:T(8,128)(2,1)} %get-tuple-element.9, bf16[3072,1536]{1,0:T(8,128)(2,1)} %get-tuple-element.10), kind=kOutput, calls=%fused_computation.18 | convolution fusion | flops 944013312 | bytes 19464192 | tf_op jit(solution)/shard_map/dot_general | solution.py:38
  158.1 1.9 copy.26
  160.0 2.6 %reshape.148 = bf16[4,2,18432]{2,1,0:T(2,128)(2,1)} reshape(bf16[3072,2,24]{2,1,0:T(2,128)(2,1)S(1)} %bitcast.58) | data formatting | bytes 589824
  162.6 5.0 %all-to-all-start.2 = ((bf16[4,2,18432]{2,1,0:T(2,128)(2,1)}), bf16[4,2,18432]{2,1,0:T(2,128)(2,1)S(1)}, u32[]{:S(2)}, u32[]{:S(2)}) async-start(bf16[4,2,18432]{2,1,0:T(2,128)(2,1)} %reshape.148), calls=%async_computation.2 | async-start | bytes 589824 | tf_op jit(solution)/shard_map/all_to_all | solution.py:91
  167.7 8.3 %all-to-all-done.2 = bf16[4,2,18432]{2,1,0:T(2,128)(2,1)S(1)} async-done(((bf16[4,2,18432]{2,1,0:T(2,128)(2,1)}), bf16[4,2,18432]{2,1,0:T(2,128)(2,1)S(1)}, u32[]{:S(2)}, u32[]{:S(2)}) %all-to-all-start.2) | async-done | bytes 294944 | tf_op jit(solution)/shard_map/all_to_all | solution.py:91
  176.0 3.1 %reshape.149 = bf16[3072,2,24]{2,1,0:T(2,128)(2,1)} reshape(bf16[4,2,18432]{2,1,0:T(2,128)(2,1)S(1)} %all-to-all-done.2) | data formatting | bytes 589824
  179.1 2.5 %convert_bitcast_fusion = f32[4,2,24,768]{2,1,3,0:T(2,128)S(1)} fusion(bf16[2,24,4,768]{1,0,3,2:T(2,128)(2,1)} %bitcast.59), kind=kLoop, calls=%fused_computation.19 | loop fusion | flops 147456 | bytes 884736 | tf_op jit(solution)/shard_map/convert_element_type | solution.py:92
  181.6 2.8 %copy.27 = f32[4,2,24,768]{3,2,1,0:T(8,128)} copy(f32[4,2,24,768]{2,1,3,0:T(2,128)S(1)} %convert_bitcast_fusion) | data formatting | bytes 1179648 | tf_op jit(solution)/shard_map/convert_element_type | solution.py:92
  184.4 1.2 fusion.22
  185.7 3.4 %collective-permute-start.2 = (bf16[8,1,768]{2,1,0:T(2,128)(2,1)S(1)}, bf16[8,1,768]{2,1,0:T(2,128)(2,1)S(1)}, u32[]{:S(2)}, u32[]{:S(2)}) collective-permute-start(bf16[8,1,768]{2,1,0:T(2,128)(2,1)S(1)} %get-tuple-element.8), channel_id=1, source_target_pairs={{4,0},{8,4},{12,8},{5,1},{9,5},{13,9},{6,2},{10,6},{14,10},{7,3},{... | collective-permute-start | bytes 36872 | tf_op jit(solution)/shard_map/ppermute | solution.py:18
  189.0 2.5 %collective-permute-start.1 = (bf16[8,1,768]{2,1,0:T(2,128)(2,1)S(1)}, bf16[8,1,768]{2,1,0:T(2,128)(2,1)S(1)}, u32[]{:S(2)}, u32[]{:S(2)}) collective-permute-start(bf16[8,1,768]{2,1,0:T(2,128)(2,1)S(1)} %get-tuple-element.7), channel_id=1, source_target_pairs={{0,4},{4,8},{8,12},{1,5},{5,9},{9,13},{2,6},{6,10},{10,14},{3,7},{... | collective-permute-start | bytes 36872 | tf_op jit(solution)/shard_map/ppermute | solution.py:15
  191.5 0.9 convert_select_fusion
  192.4 0.0 collective-permute-done.2
  192.4 3.2 %collective-permute-done.1 = bf16[8,1,768]{2,1,0:T(2,128)(2,1)S(1)} collective-permute-done((bf16[8,1,768]{2,1,0:T(2,128)(2,1)S(1)}, bf16[8,1,768]{2,1,0:T(2,128)(2,1)S(1)}, u32[]{:S(2)}, u32[]{:S(2)}) %collective-permute-start.1) | collective-permute-done | bytes 12320 | tf_op jit(solution)/shard_map/ppermute | solution.py:15
  195.7 0.1 maximum_convert_fusion
  195.8 2.2 %fusion.20 = f32[1,8,24,768]{3,2,1,0:T(8,128)} fusion(f32[8,26,768]{2,1,0:T(8,128)S(1)} %maximum_convert_fusion, f32[24,768]{1,0:T(8,128)S(1)} %convert_select_fusion, f32[24,768]{1,0:T(8,128)} %bitcast.65, f32[4,2,24,768]{3,2,1,0:T(8,128)} %copy.27, f32[4,24,768]{2,1,0:T(8,128)} %copy-done.1, f32[4,24,768]{2,1,0:T(8,128)S(1)} %copy.24), kind=kLoop, calls=%fused_computation.25 | loop fusion | flops 1179648 | bytes 3096576 | tf_op jit(solution)/shard_map/broadcast_in_dim | solution.py:94
  (5 shorter events, 0.1 us)
Async XLA Ops:
  0.0 139.8 %copy-start = (f32[1,8,3072]{2,1,0:T(8,128)S(1)}, f32[1,8,3072]{2,1,0:T(8,128)}, u32[]{:S(2)}) copy-start(f32[1,8,3072]{2,1,0:T(8,128)} %param.9) | copy-start | bytes 294916
  0.0 6.8 %copy-start.2 = (s32[1,1,1,16,128]{4,3,2,1,0:T(8,128)S(1)}, s32[1,1,1,16,128]{4,3,2,1,0:T(8,128)}, u32[]{:S(2)}) copy-start(s32[1,1,1,16,128]{4,3,2,1,0:T(8,128)} %param.12) | copy-start | bytes 24580
  0.0 16.3 %copy-start.3 = (f32[1,1,1,16,128]{4,3,2,1,0:T(8,128)S(1)}, f32[1,1,1,16,128]{4,3,2,1,0:T(8,128)}, u32[]{:S(2)}) copy-start(f32[1,1,1,16,128]{4,3,2,1,0:T(8,128)} %param.14) | copy-start | bytes 24580
  0.0 16.3 %copy-start.5 = (s32[1,1,1,16]{3,2,1,0:T(1,128)S(1)}, s32[1,1,1,16]{3,2,1,0:T(1,128)}, u32[]{:S(2)}) copy-start(s32[1,1,1,16]{3,2,1,0:T(1,128)} %param.15) | copy-start | bytes 196
  0.0 25.6 %copy-start.4 = (s32[1,1,1,16,128]{4,3,2,1,0:T(8,128)S(1)}, s32[1,1,1,16,128]{4,3,2,1,0:T(8,128)}, u32[]{:S(2)}) copy-start(s32[1,1,1,16,128]{4,3,2,1,0:T(8,128)} %param.13) | copy-start | bytes 24580
  1.2 54.9 %copy-start.1 = (f32[4,24,768]{2,1,0:T(8,128)}, f32[4,24,768]{2,1,0:T(8,128)S(1)}, u32[]{:S(2)}) copy-start(f32[4,24,768]{2,1,0:T(8,128)S(1)} %get-tuple-element.6) | copy-start | bytes 884740
  16.4 1.3 collective-permute-start
  18.3 13.4 %all-to-all-start = ((f32[16,4,128]{2,1,0:T(4,128)}), f32[16,4,128]{2,1,0:T(4,128)S(1)}, u32[]{:S(2)}, u32[]{:S(2)}) async-start(f32[16,4,128]{2,1,0:T(4,128)} %copy.22), calls=%async_computation | async-start | bytes 65536 | tf_op jit(solution)/shard_map/all_to_all | solution.py:83
  56.8 83.0 %all-to-all-start.1 = ((bf16[8,24,768]{2,1,0:T(8,128)(2,1)}), bf16[8,24,768]{2,1,0:T(8,128)(2,1)S(1)}, u32[]{:S(2)}, u32[]{:S(2)}) async-start(bf16[8,24,768]{2,1,0:T(8,128)(2,1)} %fusion.21), calls=%async_computation.1 | async-start | bytes 589824 | tf_op jit(solution)/shard_map/all_to_all | solution.py:89
  162.6 13.3 %all-to-all-start.2 = ((bf16[4,2,18432]{2,1,0:T(2,128)(2,1)}), bf16[4,2,18432]{2,1,0:T(2,128)(2,1)S(1)}, u32[]{:S(2)}, u32[]{:S(2)}) async-start(bf16[4,2,18432]{2,1,0:T(2,128)(2,1)} %reshape.148), calls=%async_computation.2 | async-start | bytes 589824 | tf_op jit(solution)/shard_map/all_to_all | solution.py:91
  185.7 6.8 %collective-permute-start.2 = (bf16[8,1,768]{2,1,0:T(2,128)(2,1)S(1)}, bf16[8,1,768]{2,1,0:T(2,128)(2,1)S(1)}, u32[]{:S(2)}, u32[]{:S(2)}) collective-permute-start(bf16[8,1,768]{2,1,0:T(2,128)(2,1)S(1)} %get-tuple-element.8), channel_id=1, source_target_pairs={{4,0},{8,4},{12,8},{5,1},{9,5},{13,9},{6,2},{10,6},{14,10},{7,3},{... | collective-permute-start | bytes 36872 | tf_op jit(solution)/shard_map/ppermute | solution.py:18
  189.0 6.6 %collective-permute-start.1 = (bf16[8,1,768]{2,1,0:T(2,128)(2,1)S(1)}, bf16[8,1,768]{2,1,0:T(2,128)(2,1)S(1)}, u32[]{:S(2)}, u32[]{:S(2)}) collective-permute-start(bf16[8,1,768]{2,1,0:T(2,128)(2,1)S(1)} %get-tuple-element.7), channel_id=1, source_target_pairs={{0,4},{4,8},{8,12},{1,5},{5,9},{9,13},{2,6},{6,10},{10,14},{3,7},{... | collective-permute-start | bytes 36872 | tf_op jit(solution)/shard_map/ppermute | solution.py:15
where the time goes:
time: 199 us; the launch traced here: 198 us
  other arithmetic  105 us (53%)
  local copies, waits for them, and re-layouts  34.5 us (17%)
  starting transfers between devices  21.7 us (11%)
  waiting for transfers between devices  18.8 us (9%)
  matrix products  17.8 us (9%)
    another operation x1, other arithmetic  79.5 us
    scatter-add x1, other arithmetic, local(): surface = surface.at[:, dst_idx].add(incoming)  17.6 us
    dot_general x1, matrix products, back_transform(): lax.dot_general(filtered, table_part, (((1,), (1,)), ((), ())), preferred...  9.63 us
    gather x2, local copies, waits for them, and re-layouts, local(): outgoing = jnp.transpose(surface[:, src_idx] * weights[None], (1, 0, 2))  9.47 us
    all_to_all x1, waiting for transfers between devices, local(): incr = lax.all_to_all(incr, 'gy', split_axis=2, concat_axis=0, tiled=True)  8.3 us
    dot_general x1, matrix products, circle_increment(): jnp.dot(circles.reshape(-1, cols_all), table, preferred_element_type=jnp....  8.22 us
    all_to_all x1, starting transfers between devices, local(): lax.all_to_all(crossed, ('gx', 'gy'), split_axis=0, concat_axis=0, tiled=...  7.28 us
    slice x2, local copies, waits for them, and re-layouts, local(): surface = fields[:FC].reshape(FC, cells)  6.78 us
  transfers between devices with their start and end apart: 6, of which 4 were waited for; matrix products, arithmetic and copies ran while one was open for 41% of the time, Pallas kernels for 0%

commit v1 on v0

--- a/solution.py
+++ b/solution.py
@@ -3,6 +3,7 @@
 import jax.numpy as jnp
 from jax import lax
 from jax.sharding import PartitionSpec as P
+from jax.lax import all_to_all, axis_size
 
 FC = 4
 
@@ -88,7 +89,19 @@
     grid_bf = fields.astype(jnp.bfloat16)
     circles = lax.all_to_all(grid_bf, "gy", split_axis=0, concat_axis=2, tiled=True)
     incr = circle_increment(circles, resp_mine, table, scale)
-    incr = lax.all_to_all(incr, "gy", split_axis=2, concat_axis=0, tiled=True)
+
+    def _unite_sheets(slab_in):
+        return jnp.concatenate(
+            all_to_all(
+                jnp.stack(jnp.split(slab_in, axis_size("gy"), axis=2)),
+                axis_name="gy",
+                split_axis=0,
+                concat_axis=0,
+            ),
+            axis=0,
+        )
+
+    incr = _unite_sheets(incr)
     fields = fields + incr.astype(jnp.float32)
     fields = diffuse(fields, rate) * keep[None]
     return fields[None]

time: 199 us -> 184 us (0.925)
  local copies, waits for them, and re-layouts: 34.5 us -> 24.1 us
  other arithmetic: 105 us -> 100 us
    unnamed x14, local copies, waits for them, and re-layouts: 5.79 us -> 0.03 us
    convert_element_type x1 -> x0, local copies, waits for them, and re-layouts: 2.83 us -> none  [local(): fields = fields + incr.astype(jnp.float32)]
    convert_element_type x1 -> x0, other arithmetic: 2.49 us -> none  [local(): fields = fields + incr.astype(jnp.float32)]
    another operation x1 -> x2, other arithmetic: 79.5 us -> 80.3 us
  transfers between devices with their start and end apart: 6 -> 6, of which waited for: 4 -> 4; matrix products, arithmetic and copies ran while one was open for 41% -> 43% of each run, Pallas kernels for 0% -> 0%
where the time goes in v1:
time: 184 us
  other arithmetic  100 us (54%)
  local copies, waits for them, and re-layouts  24.1 us (13%)
  starting transfers between devices  21.7 us (12%)
  waiting for transfers between devices  19.7 us (11%)
  matrix products  17.9 us (10%)
    another operation x1, other arithmetic  79.6 us
    scatter-add x1, other arithmetic, local(): surface = surface.at[:, dst_idx].add(incoming)  17.6 us
    dot_general x1, matrix products, back_transform(): lax.dot_general(filtered, table_part, (((1,), (1,)), ((), ())), preferred...  9.66 us
    gather x2, local copies, waits for them, and re-layouts, local(): outgoing = jnp.transpose(surface[:, src_idx] * weights[None], (1, 0, 2))  9.47 us
    all_to_all x1, waiting for transfers between devices, _unite_sheets(): all_to_all(jnp.stack(jnp.split(slab_in, axis_size('gy'), axis=2)), axis_n...  8.3 us
    dot_general x1, matrix products, circle_increment(): jnp.dot(circles.reshape(-1, cols_all), table, preferred_element_type=jnp....  8.21 us
    all_to_all x1, starting transfers between devices, local(): lax.all_to_all(crossed, ('gx', 'gy'), split_axis=0, concat_axis=0, tiled=...  7.28 us
    slice x2, local copies, waits for them, and re-layouts, local(): surface = fields[:FC].reshape(FC, cells)  6.81 us
  transfers between devices with their start and end apart: 6, of which 4 were waited for; matrix products, arithmetic and copies ran while one was open for 43% of the time, Pallas kernels for 0%

profile of v1, /device:TPU:4, one launch (start us, length us, event | category | flops | bytes accessed | tf_op | source)
XLA Modules:
  0.0 183.6 jit_solution(3160368851103368044)
XLA Ops:
  0.0 0.0 copy-start
  0.0 0.0 copy-start.3
  0.0 0.0 copy-start.4
  0.0 0.0 copy-start.6
  0.0 0.0 copy-start.5
  0.0 1.1 fusion.28
  1.2 5.7 %copy.17 = f32[1,4,24,768]{1,3,2,0:T(8,128)} copy(f32[1,4,24,768]{3,2,1,0:T(8,128)S(1)} %get-tuple-element.5) | data formatting | bytes 589824 | tf_op jit(solution)/shard_map/slice | solution.py:81
  6.8 0.0 copy-done.3
  6.9 9.1 %gather_fusion = f32[2048,4]{1,0:T(8,128)S(1)} fusion(f32[4,18432]{0,1:T(8,128)} %bitcast.55, s32[2048]{0:T(1024)S(1)} %fusion.25), kind=kCustom, calls=%fused_computation | custom fusion | bytes 73728 | tf_op jit(solution)/shard_map/gather | solution.py:82
  16.0 0.3 copy.18
  16.3 0.0 copy-done.4
  16.3 0.0 copy-done.6
  16.3 0.1 bitcast_select_fusion
  16.4 0.1 collective-permute-start
  16.5 1.2 collective-permute-done
  17.7 0.6 copy.19
  18.3 7.3 %all-to-all-start = ((f32[16,4,128]{2,1,0:T(4,128)}), f32[16,4,128]{2,1,0:T(4,128)S(1)}, u32[]{:S(2)}, u32[]{:S(2)}) async-start(f32[16,4,128]{2,1,0:T(4,128)} %copy.19), calls=%async_computation | async-start | bytes 65536 | tf_op jit(solution)/shard_map/all_to_all | solution.py:84
  25.6 0.0 copy-done.5
  25.6 6.1 %all-to-all-done = f32[16,4,128]{2,1,0:T(4,128)S(1)} async-done(((f32[16,4,128]{2,1,0:T(4,128)}), f32[16,4,128]{2,1,0:T(4,128)S(1)}, u32[]{:S(2)}, u32[]{:S(2)}) %all-to-all-start) | async-done | bytes 32800 | tf_op jit(solution)/shard_map/all_to_all | solution.py:84
  31.7 0.4 copy.20
  32.1 17.6 %scatter_fusion = f32[4,18432]{0,1:T(8,128)} fusion(f32[4,18432]{0,1:T(8,128)} %bitcast.56, s32[2048]{0:T(1024)S(1)} %fusion.23, f32[2048,4]{1,0:T(8,128)S(1)} %copy.20), kind=kCustom, calls=%fused_computation.1 | custom fusion | flops 8192 | bytes 106496 | tf_op jit(solution)/shard_map/scatter-add | solution.py:86
  49.7 6.4 %copy.21 = f32[4,24,768]{2,1,0:T(8,128)S(1)} copy(f32[4,24,768]{0,2,1:T(8,128)} %bitcast.57) | data formatting | bytes 589824 | tf_op jit(solution)/shard_map/reshape | solution.py:87
  56.1 0.8 fusion.21
  56.8 3.5 %all-to-all-start.1 = ((bf16[8,24,768]{2,1,0:T(8,128)(2,1)}), bf16[8,24,768]{2,1,0:T(8,128)(2,1)S(1)}, u32[]{:S(2)}, u32[]{:S(2)}) async-start(bf16[8,24,768]{2,1,0:T(8,128)(2,1)} %fusion.21), calls=%async_computation.1 | async-start | bytes 589824 | tf_op jit(solution)/shard_map/all_to_all | solution.py:90
  60.3 79.6 %sine_convert_fusion = (bf16[3072,1536]{1,0:T(8,128)(2,1)}, bf16[3072,1536]{1,0:T(8,128)(2,1)}) fusion(), kind=kLoop, calls=%fused_computation.8 | loop fusion | flops 51904512 | bytes 18874368 | tf_op jit(solution)/shard_map/convert.2
  139.9 0.0 copy-done
  139.9 0.0 all-to-all-done.1
  139.9 0.2 copy.24
  140.1 0.2 dot_general.8
  140.3 8.2 %fusion.12 = bf16[2,24,3072]{2,1,0:T(8,128)(2,1)S(1)} fusion(bf16[2,24,3072]{2,1,0:T(8,128)(2,1)S(1)} %dot_general.8, bf16[3072,1536]{1,0:T(8,128)(2,1)} %get-tuple-element.13, bf16[3072,1536]{1,0:T(8,128)(2,1)} %get-tuple-element.14, f32[2,3072]{1,0:T(2,128)S(1)} %dynamic-slice_bitcast_fusion), kind=kOutput, calls=%fused_computation.17 | convolution fusion | flops 944013312 | bytes 19488768 | tf_op jit(solution)/shard_map/dot_general | solution.py:46
  148.5 0.0 copy-start.2
  148.5 0.0 copy-start.1
  148.5 9.7 %fusion.15 = bf16[48,3072]{1,0:T(8,128)(2,1)S(1)} fusion(bf16[48,3072]{1,0:T(8,128)(2,1)S(1)} %bitcast.65, bf16[3072,1536]{1,0:T(8,128)(2,1)} %get-tuple-element.13, bf16[3072,1536]{1,0:T(8,128)(2,1)} %get-tuple-element.14), kind=kOutput, calls=%fused_computation.18 | convolution fusion | flops 944013312 | bytes 19464192 | tf_op jit(solution)/shard_map/dot_general | solution.py:39
  158.2 0.8 pad_maximum_fusion.8
  159.0 5.1 %all-to-all-start.2 = ((bf16[4,2,24,768]{3,2,1,0:T(8,128)(2,1)}), bf16[4,2,24,768]{3,2,1,0:T(8,128)(2,1)S(1)}, u32[]{:S(2)}, u32[]{:S(2)}) async-start(bf16[4,2,24,768]{3,2,1,0:T(8,128)(2,1)} %pad_maximum_fusion.8), calls=%async_computation.2 | async-start | bytes 589824 | tf_op jit(solution)/shard_map/all_to_all | solution.py:95
  164.0 8.3 %all-to-all-done.2 = bf16[4,2,24,768]{3,2,1,0:T(8,128)(2,1)S(1)} async-done(((bf16[4,2,24,768]{3,2,1,0:T(8,128)(2,1)}), bf16[4,2,24,768]{3,2,1,0:T(8,128)(2,1)S(1)}, u32[]{:S(2)}, u32[]{:S(2)}) %all-to-all-start.2) | async-done | bytes 294944 | tf_op jit(solution)/shard_map/all_to_all | solution.py:95
  172.3 0.1 fusion.22
  172.5 3.4 %collective-permute-start.2 = (bf16[8,1,768]{2,1,0:T(2,128)(2,1)S(1)}, bf16[8,1,768]{2,1,0:T(2,128)(2,1)S(1)}, u32[]{:S(2)}, u32[]{:S(2)}) collective-permute-start(bf16[8,1,768]{2,1,0:T(2,128)(2,1)S(1)} %get-tuple-element.8), channel_id=1, source_target_pairs={{4,0},{8,4},{12,8},{5,1},{9,5},{13,9},{6,2},{10,6},{14,10},{7,3},{... | collective-permute-start | bytes 36872 | tf_op jit(solution)/shard_map/ppermute | solution.py:19
  175.8 2.5 %collective-permute-start.1 = (bf16[8,1,768]{2,1,0:T(2,128)(2,1)S(1)}, bf16[8,1,768]{2,1,0:T(2,128)(2,1)S(1)}, u32[]{:S(2)}, u32[]{:S(2)}) collective-permute-start(bf16[8,1,768]{2,1,0:T(2,128)(2,1)S(1)} %get-tuple-element.7), channel_id=1, source_target_pairs={{0,4},{4,8},{8,12},{1,5},{5,9},{9,13},{2,6},{6,10},{10,14},{3,7},{... | collective-permute-start | bytes 36872 | tf_op jit(solution)/shard_map/ppermute | solution.py:16
  178.3 0.0 copy-done.2
  178.3 0.0 collective-permute-done.2
  178.4 4.1 %collective-permute-done.1 = bf16[8,1,768]{2,1,0:T(2,128)(2,1)S(1)} collective-permute-done((bf16[8,1,768]{2,1,0:T(2,128)(2,1)S(1)}, bf16[8,1,768]{2,1,0:T(2,128)(2,1)S(1)}, u32[]{:S(2)}, u32[]{:S(2)}) %collective-permute-start.1) | collective-permute-done | bytes 12320 | tf_op jit(solution)/shard_map/ppermute | solution.py:16
  182.5 0.1 maximum_convert_fusion
  182.6 0.0 copy-done.1
  182.6 1.0 fusion.20
  (7 shorter events, 0.1 us)
Async XLA Ops:
  0.0 139.9 %copy-start = (f32[1,8,3072]{2,1,0:T(8,128)S(1)}, f32[1,8,3072]{2,1,0:T(8,128)}, u32[]{:S(2)}) copy-start(f32[1,8,3072]{2,1,0:T(8,128)} %param.9) | copy-start | bytes 294916
  0.0 6.8 %copy-start.3 = (s32[1,1,1,16,128]{4,3,2,1,0:T(8,128)S(1)}, s32[1,1,1,16,128]{4,3,2,1,0:T(8,128)}, u32[]{:S(2)}) copy-start(s32[1,1,1,16,128]{4,3,2,1,0:T(8,128)} %param.12) | copy-start | bytes 24580
  0.0 16.3 %copy-start.4 = (f32[1,1,1,16,128]{4,3,2,1,0:T(8,128)S(1)}, f32[1,1,1,16,128]{4,3,2,1,0:T(8,128)}, u32[]{:S(2)}) copy-start(f32[1,1,1,16,128]{4,3,2,1,0:T(8,128)} %param.14) | copy-start | bytes 24580
  0.0 16.3 %copy-start.6 = (s32[1,1,1,16]{3,2,1,0:T(1,128)S(1)}, s32[1,1,1,16]{3,2,1,0:T(1,128)}, u32[]{:S(2)}) copy-start(s32[1,1,1,16]{3,2,1,0:T(1,128)} %param.15) | copy-start | bytes 196
  0.0 25.6 %copy-start.5 = (s32[1,1,1,16,128]{4,3,2,1,0:T(8,128)S(1)}, s32[1,1,1,16,128]{4,3,2,1,0:T(8,128)}, u32[]{:S(2)}) copy-start(s32[1,1,1,16,128]{4,3,2,1,0:T(8,128)} %param.13) | copy-start | bytes 24580
  16.4 1.3 collective-permute-start
  18.3 13.4 %all-to-all-start = ((f32[16,4,128]{2,1,0:T(4,128)}), f32[16,4,128]{2,1,0:T(4,128)S(1)}, u32[]{:S(2)}, u32[]{:S(2)}) async-start(f32[16,4,128]{2,1,0:T(4,128)} %copy.19), calls=%async_computation | async-start | bytes 65536 | tf_op jit(solution)/shard_map/all_to_all | solution.py:84
  56.8 83.1 %all-to-all-start.1 = ((bf16[8,24,768]{2,1,0:T(8,128)(2,1)}), bf16[8,24,768]{2,1,0:T(8,128)(2,1)S(1)}, u32[]{:S(2)}, u32[]{:S(2)}) async-start(bf16[8,24,768]{2,1,0:T(8,128)(2,1)} %fusion.21), calls=%async_computation.1 | async-start | bytes 589824 | tf_op jit(solution)/shard_map/all_to_all | solution.py:90
  148.5 29.8 %copy-start.2 = (s32[24,768]{1,0:T(8,128)S(1)}, s32[24,768]{1,0:T(8,128)}, u32[]{:S(2)}) copy-start(s32[24,768]{1,0:T(8,128)} %param.11) | copy-start | bytes 221188
  148.5 34.1 %copy-start.1 = (f32[1,24,768]{2,1,0:T(8,128)S(1)}, f32[1,24,768]{2,1,0:T(8,128)}, u32[]{:S(2)}) copy-start(f32[1,24,768]{2,1,0:T(8,128)} %param.10) | copy-start | bytes 221188
  159.0 13.4 %all-to-all-start.2 = ((bf16[4,2,24,768]{3,2,1,0:T(8,128)(2,1)}), bf16[4,2,24,768]{3,2,1,0:T(8,128)(2,1)S(1)}, u32[]{:S(2)}, u32[]{:S(2)}) async-start(bf16[4,2,24,768]{3,2,1,0:T(8,128)(2,1)} %pad_maximum_fusion.8), calls=%async_computation.2 | async-start | bytes 589824 | tf_op jit(solution)/shard_map/all_to_all | solution.py:95
  172.5 5.9 %collective-permute-start.2 = (bf16[8,1,768]{2,1,0:T(2,128)(2,1)S(1)}, bf16[8,1,768]{2,1,0:T(2,128)(2,1)S(1)}, u32[]{:S(2)}, u32[]{:S(2)}) collective-permute-start(bf16[8,1,768]{2,1,0:T(2,128)(2,1)S(1)} %get-tuple-element.8), channel_id=1, source_target_pairs={{4,0},{8,4},{12,8},{5,1},{9,5},{13,9},{6,2},{10,6},{14,10},{7,3},{... | collective-permute-start | bytes 36872 | tf_op jit(solution)/shard_map/ppermute | solution.py:19
  175.8 6.6 %collective-permute-start.1 = (bf16[8,1,768]{2,1,0:T(2,128)(2,1)S(1)}, bf16[8,1,768]{2,1,0:T(2,128)(2,1)S(1)}, u32[]{:S(2)}, u32[]{:S(2)}) collective-permute-start(bf16[8,1,768]{2,1,0:T(2,128)(2,1)S(1)} %get-tuple-element.7), channel_id=1, source_target_pairs={{0,4},{4,8},{8,12},{1,5},{5,9},{9,13},{2,6},{6,10},{10,14},{3,7},{... | collective-permute-start | bytes 36872 | tf_op jit(solution)/shard_map/ppermute | solution.py:16
